TPU v7x, 512 devices: a whole 4x8x8 slice. The times are simulated.
512 devices in a mesh: dp: 8 (over z_lo, core), ctx: 64 (over z_hi, y, x).
Axes of the slice: x: 4, y: 8, z: 8 (z_hi: 2, z_lo: 4; z = z_hi * 4 + z_lo), core: 2. Of those that a mesh axis runs over, the one named last changes fastest.
Arguments:
- queries: bfloat16 [32768, 4096], P(('dp', 'ctx')), parts along dimension 0, as said below
- keys: bfloat16 [32768, 512], P(('dp', 'ctx')), parts along dimension 0, as said below
- values: bfloat16 [32768, 512], P(('dp', 'ctx')), parts along dimension 0, may hold values from -6 to 6
Outputs:
- attended: bfloat16 [32768, 4096], P(('dp', 'ctx')), parts along dimension 0
There are 8 independent parts, one for each index of `dp`. A program takes and returns all parts, laid end to end along the dimension named above; each array names one. Nothing has to cross between parts.
Inputs may be any that keep to these rules, and one draw needn't show every extreme that they name: `queries`: entries lie between -310 / sqrt(128) and 310 / sqrt(128). `keys`: entries lie between -6 and 6.
All inputs are finite; a program needn't handle non-finite values.
Results may differ from a plain program's by a relative error of at most 0.0035.
Values may be sent and summed in bfloat16 or wider, within the bound.
No kernel may reach another device: no remote copies, remote signals or barrier semaphores. Data moves between devices by JAX's collectives and lax.ppermute only.
A program may use at most 128 MiB of HBM per device.

v0:
```python
import math
import jax
import jax.numpy as jnp
from jax import lax
from jax.sharding import PartitionSpec as P

QH = 32
KVH = 4
HD = 128


def fresh_state(length, group_size):
    return (
        jnp.zeros((length, KVH, group_size, HD), jnp.float32),
        jnp.full((KVH, group_size, length), -1e30, jnp.float32),
        jnp.zeros((KVH, group_size, length), jnp.float32),
    )


def absorb(carry_state, query_block, query_pos, key_piece, value_piece):
    summed, running_max, denominator = carry_state
    key_heads = key_piece.reshape(key_piece.shape[0], KVH, HD)
    value_heads = value_piece.reshape(value_piece.shape[0], KVH, HD)
    scores = jnp.einsum(
        "tkgd,skd->kgts", query_block, key_heads, preferred_element_type=jnp.float32
    )
    scores = scores * (1.0 / math.sqrt(HD))
    key_pos = jnp.arange(key_heads.shape[0], dtype=jnp.int32)
    scores = jnp.where(key_pos[None, :] <= query_pos[:, None], scores, -jnp.inf)
    new_max = jnp.maximum(running_max, scores.max(-1))
    weights = jnp.exp(scores - new_max[..., None])
    denominator = weights.sum(-1)
    mixed_values = jnp.einsum(
        "kgts,skd->tkgd",
        weights.astype(jnp.bfloat16),
        value_heads,
        preferred_element_type=jnp.float32,
    )
    summed = mixed_values
    return (summed, new_max, denominator)


def guarded(carry_state, query_block, query_pos, key_piece, value_piece, offset):
    return lax.cond(
        offset <= query_pos[-1],
        lambda kept: absorb(kept, query_block, query_pos, key_piece, value_piece),
        lambda kept: kept,
        carry_state,
    )


def finish(carry_state):
    summed, running_max, denominator = carry_state
    result = summed / jnp.transpose(denominator, (2, 0, 1))[..., None]
    return result.reshape(summed.shape[0], QH * HD).astype(jnp.bfloat16)


def local(queries, keys, values):
    local_rows = queries.shape[0]
    my_index = lax.axis_index("ctx")
    group_size = QH // KVH
    own_pos = my_index * local_rows + jnp.arange(local_rows, dtype=jnp.int32)
    query_sets = ((queries.reshape(local_rows, KVH, group_size, HD), own_pos),)
    initial = tuple((fresh_state(entry[1].shape[0], group_size) for entry in query_sets))
    pieces = (
        lax.all_gather(keys, "ctx", axis=0, tiled=True),
        lax.all_gather(values, "ctx", axis=0, tiled=True),
    )
    offset = jnp.int32(0)
    states = tuple(
        (
            guarded(
                initial[number],
                query_sets[number][0],
                query_sets[number][1],
                pieces[0],
                pieces[1],
                offset,
            )
            for number in range(len(query_sets))
        )
    )
    return finish(states[0])


def solution(mesh):
    in_specs = (P(("dp", "ctx"), None), P(("dp", "ctx"), None), P(("dp", "ctx"), None))
    out_specs = P(("dp", "ctx"), None)
    return jax.shard_map(local, mesh=mesh, in_specs=in_specs, out_specs=out_specs, check_vma=False)
```

profile of v0, /device:TPU:2, one launch (start us, length us, event | category | flops | bytes accessed | tf_op | source)
XLA Modules:
  0.0 402.2 jit_solution(12471639932094628450)
XLA Ops:
  6.5 0.0 all-gather.3.cloned.1.call-start
  6.5 0.7 all-gather.3.cloned.1.call-update
  7.3 0.0 all-gather.5.cloned.1.call-start
  7.3 0.7 all-gather.5.cloned.1.call-update
  8.0 0.6 slice.3
  9.3 164.9 %all-gather.3.cloned.1.call-done = bf16[4096,512]{1,0:T(8,128)(2,1)} async-done(((bf16[64,512]{1,0:T(8,128)(2,1)}), bf16[4096,512]{1,0:T(8,128)(2,1)}) %all-gather.3.cloned.1.call-update) | async-done | bytes 4194320 | tf_op jit(solution)/shard_map/all_gather | solution.py:66
  174.2 156.1 %all-gather.5.cloned.1.call-done = bf16[4096,512]{1,0:T(8,128)(2,1)} async-done(((bf16[64,512]{1,0:T(8,128)(2,1)}), bf16[4096,512]{1,0:T(8,128)(2,1)}) %all-gather.5.cloned.1.call-update) | async-done | bytes 4194320 | tf_op jit(solution)/shard_map/all_gather | solution.py:67
  330.3 63.4 %conditional.1 = (f32[64,4,8,128]{3,0,2,1:T(8,128)S(1)}, f32[4,8,64]{2,1,0:T(8,128)S(1)}) conditional(s32[]{:T(128)} %bitcast.4, () %tuple.13, (s32[64]{0:T(128)S(1)}, bf16[4096,512]{1,0:T(8,128)(2,1)}, bf16[64,4096]{1,0:T(8,128)(2,1)}, bf16[4096,512]{1,0:T(8,128)(2,1)}) %tuple.14), branch_computations={%region_0.0_spmd, %region_1.4_spmd} | conditional | flops 4387502080 | bytes 129548560 | solution.py:44
  330.3 0.2 iota_compare_fusion
  330.5 6.9 %reshape.18 = bf16[4096,4,128]{2,1,0:T(4,128)(2,1)} reshape(bf16[4096,512]{1,0:T(8,128)(2,1)} %get-tuple-element.15) | data formatting | bytes 8388608 | tf_op jit(solution)/shard_map/cond/branch_1_fun/reshape | solution.py:22
  337.4 1.1 copy.15
  338.5 16.7 %fusion.2 = (f32[4,8,64]{2,1,0:T(8,128)S(1)}, f32[4,4096,64,8]{1,2,3,0:T(8,128)}) fusion(pred[64,4096]{1,0:T(8,128)(4,1)S(1)} %iota_compare_fusion, bf16[64,4,8,128]{3,2,1,0:T(8,128)(2,1)S(1)} %bitcast.27, bf16[4096,4,128,1]{2,1,0,3:T(4,128)(2,1)} %bitcast.25), kind=kOutput, calls=%fused_computation.4 | convolution fusion | flops 2172647424 | bytes 38543360 | tf_op jit(solution)/shard_map/cond/branch_1_fun/tkgd,skd->kgts/dot_general | solution.py:24
  355.2 15.4 %fusion = f32[4,8,64]{2,1,0:T(8,128)S(1)} fusion(f32[4,4096,64,8]{1,2,3,0:T(8,128)} %get-tuple-element.25, f32[4,8,64]{2,1,0:T(8,128)S(1)} %broadcast_maximum_fusion, pred[64,4096]{1,0:T(8,128)(4,1)S(1)} %iota_compare_fusion), kind=kLoop, calls=%fused_computation.2 | loop fusion | flops 33552384 | bytes 33832960 | tf_op jit(solution)/shard_map/cond/branch_1_fun/reduce_sum | solution.py:32
  370.5 6.9 %reshape.20 = bf16[4096,4,128]{2,1,0:T(4,128)(2,1)} reshape(bf16[4096,512]{1,0:T(8,128)(2,1)} %get-tuple-element.17) | data formatting | bytes 8388608 | tf_op jit(solution)/shard_map/cond/branch_1_fun/reshape | solution.py:23
  377.4 16.3 %fusion.9 = f32[64,4,8,128]{3,0,2,1:T(8,128)S(1)} fusion(bf16[4096,4,128,1]{2,1,0,3:T(4,128)(2,1)} %bitcast.26, f32[4,4096,64,8]{1,2,3,0:T(8,128)} %get-tuple-element.25, f32[4,8,64]{2,1,0:T(8,128)S(1)} %broadcast_maximum_fusion, pred[64,4096]{1,0:T(8,128)(4,1)S(1)} %iota_compare_fusion), kind=kOutput, calls=%fused_computation.10 | convolution fusion | flops 2181038080 | bytes 39067648 | tf_op jit(solution)/shard_map/cond/branch_1_fun/kgts,skd->tkgd/dot_general | solution.py:33
  393.7 0.3 divide_convert_fusion
  394.0 0.3 copy.8
  394.4 1.0 copy.30
  (2 shorter events, 0.0 us)
Async XLA Ops:
  6.5 167.6 %all-gather.3.cloned.1.call-start = ((), (), s32[]{:S(2)}) async-start(), calls=%async_computation | async-start | bytes 4259840 | tf_op jit(solution)/shard_map/all_gather | solution.py:66
  7.3 323.0 %all-gather.5.cloned.1.call-start = ((), (), s32[]{:S(2)}) async-start(), calls=%async_computation.1 | async-start | bytes 4259840 | tf_op jit(solution)/shard_map/all_gather | solution.py:67
Sparse Core Ops, SparseCore 0:
  11.8 162.2 all-gather.2
  178.7 151.5 all-gather.4
where the time goes:
time: 403 us; the launch traced here: 402 us
  waiting for transfers between devices  322 us (80%)
  matrix products  32.9 us (8%)
  local copies, waits for them, and re-layouts  16.8 us (4%)
  other arithmetic  15.9 us (4%)
  between operations  14.1 us (3%)
    all_gather x1, waiting for transfers between devices, local(): lax.all_gather(keys, 'ctx', axis=0, tiled=True)  165 us
    all_gather x1, waiting for transfers between devices, local(): lax.all_gather(values, 'ctx', axis=0, tiled=True)  156 us
    dot_general x1, matrix products, absorb(): jnp.einsum('tkgd,skd->kgts', query_block, key_heads, preferred_element_ty...  16.7 us
    dot_general x1, matrix products, absorb(): jnp.einsum('kgts,skd->tkgd', weights.astype(jnp.bfloat16), value_heads, p...  16.3 us
    reduce_sum x1, other arithmetic, absorb(): denominator = weights.sum(-1)  15.4 us
  transfers between devices with their start and end apart: 2, of which 2 were waited for; matrix products, arithmetic and copies ran while one was open for 0% of the time, Pallas kernels for 0%

commit v1 on v0

--- a/solution.py
+++ b/solution.py
@@ -64,7 +64,15 @@
     initial = tuple((fresh_state(entry[1].shape[0], group_size) for entry in query_sets))
     pieces = (
         lax.all_gather(keys, "ctx", axis=0, tiled=True),
-        lax.all_gather(values, "ctx", axis=0, tiled=True),
+        jnp.concatenate(
+            jax.lax.all_to_all(
+                jnp.stack([values for _ in range(jax.lax.psum(1, axis_name="ctx"))]),
+                axis_name="ctx",
+                split_axis=0,
+                concat_axis=0,
+            ),
+            axis=0,
+        ),
     )
     offset = jnp.int32(0)
     states = tuple(

time: 403 us -> 331 us (0.82)
  waiting for transfers between devices: 322 us -> 228 us
  starting transfers between devices: 0.04 us -> 19.3 us
    all_gather x1 -> x0, waiting for transfers between devices: 156 us -> none  [local(): lax.all_gather(values, 'ctx', axis=0, tiled=True)]
    all_to_all x0 -> x1, waiting for transfers between devices: none -> 104 us  [local(): jax.lax.all_to_all(jnp.stack([values for _ in range(jax.lax.psum(1, axis_...]
    all_gather x1, waiting for transfers between devices: 165 us -> 124 us  [local(): lax.all_gather(keys, 'ctx', axis=0, tiled=True)]
    all_to_all x0 -> x1, starting transfers between devices: none -> 19.3 us  [local(): jax.lax.all_to_all(jnp.stack([values for _ in range(jax.lax.psum(1, axis_...]
    another operation x0 -> x2, local copies, waits for them, and re-layouts: none -> 10.2 us  [the longest x1 6.88 us: absorb(): value_heads = value_piece.reshape(value_piece.shape[0], KVH, HD)]
    reshape x1 -> x0, local copies, waits for them, and re-layouts: 6.87 us -> none  [absorb(): value_heads = value_piece.reshape(value_piece.shape[0], KVH, HD)]
where the time goes in v1:
time: 331 us
  waiting for transfers between devices  228 us (69%)
  matrix products  32.9 us (10%)
  local copies, waits for them, and re-layouts  20.1 us (6%)
  starting transfers between devices  19.3 us (6%)
  other arithmetic  15.9 us (5%)
  between operations  14.1 us (4%)
    all_gather x1, waiting for transfers between devices, local(): lax.all_gather(keys, 'ctx', axis=0, tiled=True)  124 us
    all_to_all x1, waiting for transfers between devices, local(): jax.lax.all_to_all(jnp.stack([values for _ in range(jax.lax.psum(1, axis_...  104 us
    all_to_all x1, starting transfers between devices, local(): jax.lax.all_to_all(jnp.stack([values for _ in range(jax.lax.psum(1, axis_...  19.3 us
    dot_general x1, matrix products, absorb(): jnp.einsum('tkgd,skd->kgts', query_block, key_heads, preferred_element_ty...  16.6 us
    dot_general x1, matrix products, absorb(): jnp.einsum('kgts,skd->tkgd', weights.astype(jnp.bfloat16), value_heads, p...  16.2 us
    reduce_sum x1, other arithmetic, absorb(): denominator = weights.sum(-1)  15.4 us
    reshape x1, local copies, waits for them, and re-layouts, absorb(): key_heads = key_piece.reshape(key_piece.shape[0], KVH, HD)  6.89 us
    another operation x1, local copies, waits for them, and re-layouts, absorb(): value_heads = value_piece.reshape(value_piece.shape[0], KVH, HD)  6.88 us
  transfers between devices with their start and end apart: 2, of which 2 were waited for; matrix products, arithmetic and copies ran while one was open for 0% of the time, Pallas kernels for 0%

profile of v1, /device:TPU:2, one launch (start us, length us, event | category | flops | bytes accessed | tf_op | source)
XLA Modules:
  0.0 330.6 jit_solution(17113282226564909740)
XLA Ops:
  6.5 3.3 stack.2
  9.8 19.3 %all-to-all-start = ((bf16[64,64,512]{2,1,0:T(8,128)(2,1)}), bf16[64,64,512]{2,1,0:T(8,128)(2,1)}, u32[]{:S(2)}, u32[]{:S(2)}) async-start(bf16[64,64,512]{2,1,0:T(8,128)(2,1)} %stack.2), calls=%async_computation | async-start | bytes 8388608 | tf_op jit(solution)/shard_map/all_to_all | solution.py:68
  29.1 0.0 all-gather.2.cloned.1.call-start
  29.2 0.7 all-gather.2.cloned.1.call-update
  29.9 0.6 slice.3
  31.1 104.0 %all-to-all-done = bf16[64,64,512]{2,1,0:T(8,128)(2,1)} async-done(((bf16[64,64,512]{2,1,0:T(8,128)(2,1)}), bf16[64,64,512]{2,1,0:T(8,128)(2,1)}, u32[]{:S(2)}, u32[]{:S(2)}) %all-to-all-start) | async-done | bytes 4194336 | tf_op jit(solution)/shard_map/all_to_all | solution.py:68
  135.1 123.7 %all-gather.2.cloned.1.call-done = bf16[4096,512]{1,0:T(8,128)(2,1)} async-done(((bf16[64,512]{1,0:T(8,128)(2,1)}), bf16[4096,512]{1,0:T(8,128)(2,1)}) %all-gather.2.cloned.1.call-update) | async-done | bytes 4194320 | tf_op jit(solution)/shard_map/all_gather | solution.py:66
  258.7 63.4 %conditional.1 = (f32[64,4,8,128]{3,0,2,1:T(8,128)S(1)}, f32[4,8,64]{2,1,0:T(8,128)S(1)}) conditional(s32[]{:T(128)} %bitcast.4, () %tuple.13, (s32[64]{0:T(128)S(1)}, bf16[4096,512]{1,0:T(8,128)(2,1)}, bf16[64,4096]{1,0:T(8,128)(2,1)}, bf16[64,64,512]{2,1,0:T(8,128)(2,1)}) %tuple.14), branch_computations={%region_0.0_spmd, %region_1.4_spmd} | conditional | flops 4387502080 | bytes 129548560 | solution.py:44
  258.7 0.2 iota_compare_fusion
  258.9 6.9 %reshape.18 = bf16[4096,4,128]{2,1,0:T(4,128)(2,1)} reshape(bf16[4096,512]{1,0:T(8,128)(2,1)} %get-tuple-element.15) | data formatting | bytes 8388608 | tf_op jit(solution)/shard_map/cond/branch_1_fun/reshape | solution.py:22
  265.8 1.1 copy.15
  267.0 16.6 %fusion.2 = (f32[4,8,64]{2,1,0:T(8,128)S(1)}, f32[4,4096,64,8]{1,2,3,0:T(8,128)}) fusion(pred[64,4096]{1,0:T(8,128)(4,1)S(1)} %iota_compare_fusion, bf16[64,4,8,128]{3,2,1,0:T(8,128)(2,1)S(1)} %bitcast.27, bf16[4096,4,128,1]{2,1,0,3:T(4,128)(2,1)} %bitcast.25), kind=kOutput, calls=%fused_computation.4 | convolution fusion | flops 2172647424 | bytes 38543360 | tf_op jit(solution)/shard_map/cond/branch_1_fun/tkgd,skd->kgts/dot_general | solution.py:24
  283.6 15.4 %fusion = f32[4,8,64]{2,1,0:T(8,128)S(1)} fusion(f32[4,4096,64,8]{1,2,3,0:T(8,128)} %get-tuple-element.25, f32[4,8,64]{2,1,0:T(8,128)S(1)} %broadcast_maximum_fusion, pred[64,4096]{1,0:T(8,128)(4,1)S(1)} %iota_compare_fusion), kind=kLoop, calls=%fused_computation.2 | loop fusion | flops 33552384 | bytes 33832960 | tf_op jit(solution)/shard_map/cond/branch_1_fun/reduce_sum | solution.py:32
  299.0 6.9 %reshape_reshape.2 = bf16[4096,4,128]{2,1,0:T(4,128)(2,1)} reshape(bf16[64,64,512]{2,1,0:T(8,128)(2,1)} %get-tuple-element.17) | data formatting | bytes 8388608 | tf_op jit(solution)/shard_map/cond/branch_1_fun/reshape;reshape | solution.py:23
  305.8 16.2 %fusion.9 = f32[64,4,8,128]{3,0,2,1:T(8,128)S(1)} fusion(bf16[4096,4,128,1]{2,1,0,3:T(4,128)(2,1)} %bitcast.26, f32[4,4096,64,8]{1,2,3,0:T(8,128)} %get-tuple-element.25, f32[4,8,64]{2,1,0:T(8,128)S(1)} %broadcast_maximum_fusion, pred[64,4096]{1,0:T(8,128)(4,1)S(1)} %iota_compare_fusion), kind=kOutput, calls=%fused_computation.10 | convolution fusion | flops 2181038080 | bytes 39067648 | tf_op jit(solution)/shard_map/cond/branch_1_fun/kgts,skd->tkgd/dot_general | solution.py:33
  322.1 0.3 divide_convert_fusion
  322.4 0.3 copy.8
  322.8 1.0 copy.30
  (2 shorter events, 0.0 us)
Async XLA Ops:
  9.8 125.3 %all-to-all-start = ((bf16[64,64,512]{2,1,0:T(8,128)(2,1)}), bf16[64,64,512]{2,1,0:T(8,128)(2,1)}, u32[]{:S(2)}, u32[]{:S(2)}) async-start(bf16[64,64,512]{2,1,0:T(8,128)(2,1)} %stack.2), calls=%async_computation | async-start | bytes 8388608 | tf_op jit(solution)/shard_map/all_to_all | solution.py:68
  29.1 229.6 %all-gather.2.cloned.1.call-start = ((), (), s32[]{:S(2)}) async-start(), calls=%async_computation.1 | async-start | bytes 4259840 | tf_op jit(solution)/shard_map/all_gather | solution.py:66
Sparse Core Ops, SparseCore 0:
  34.4 224.2 all-gather.1
